TPU v7x, 32 devices: a whole 2x2x4 slice. The times are simulated.
32 devices in a mesh: row: 4 (over y, x), col: 8 (over z, core).
Axes of the slice: x: 2, y: 2, z: 4, core: 2. Of those that a mesh axis runs over, the one named last changes fastest.
Arguments:
- queries: bfloat16 [32, 128, 512], P('row', 'col'), may hold values from -6 to 6
- keys: bfloat16 [32, 128, 512], P('row', 'col'), may hold values from -6 to 6
- values: bfloat16 [32, 128, 512], P('row', 'col'), may hold values from -6 to 6
- grad_out: bfloat16 [32, 128, 512], P('row', 'col'), may hold values from -6 to 6
- rel_bias: float32 [8, 17, 17], replicated, may hold values from -4 to 4
- occupied: int32 [4, 8], replicated, may hold values 0 or 1
Outputs:
- grad_queries: bfloat16 [32, 128, 512], P('row', 'col')
- grad_keys: bfloat16 [32, 128, 512], P('row', 'col')
- grad_values: bfloat16 [32, 128, 512], P('row', 'col')
- grad_bias: float32 [8, 17, 17], replicated
All inputs are finite; a program needn't handle non-finite values.
Results may differ from a plain program's by a relative error of at most 0.015.
Values may be sent and summed in bfloat16 or wider, within the bound.
A program may use at most 64 MiB of HBM per device.

v0:
```python
import jax
import jax.numpy as jnp
from jax import lax
from jax.sharding import PartitionSpec as P


def from_behind(value, axis, steps):
    count = lax.axis_size(axis)
    first, last = (max(0, -steps), min(count, count - steps))
    return lax.ppermute(value, axis, [(source, source + steps) for source in range(first, last)])


def with_halo(block, sides, width):
    for axis, dim in sides:
        count = lax.axis_size(axis)
        forward = [(i, i + 1) for i in range(count - 1)]
        backward = [(target, source) for source, target in forward]
        low = lax.ppermute(
            lax.slice_in_dim(block, block.shape[dim] - width, None, axis=dim), axis, forward
        )
        high = lax.ppermute(lax.slice_in_dim(block, 0, width, axis=dim), axis, backward)
        block = jnp.concatenate([low, block, high], axis=dim)
    return block


def offset_table(first_count, second_count, direction, window_span):
    table_shape = (first_count, second_count, window_span)
    first_index = lax.broadcasted_iota(jnp.int32, table_shape, 0)
    second_index = lax.broadcasted_iota(jnp.int32, table_shape, 1)
    slot_index = lax.broadcasted_iota(jnp.int32, table_shape, 2)
    return (direction * (second_index - first_index) == slot_index).astype(jnp.float32)


def expand_part(table_rows, table_cols, bias_part):
    partial_bias = jnp.einsum(
        "cqe,de->cqd", table_cols, bias_part, preferred_element_type=jnp.float32
    ).astype(jnp.bfloat16)
    return jnp.einsum("rpd,cqd->rcpq", table_rows, partial_bias, preferred_element_type=jnp.float32)


def expand_bias(table_rows, table_cols, bias_head):
    rows_low = table_rows.astype(jnp.bfloat16)
    cols_low = table_cols.astype(jnp.bfloat16)
    bias_high = bias_head.astype(jnp.bfloat16)
    bias_rest = (bias_head - bias_high.astype(jnp.float32)).astype(jnp.bfloat16)
    full_bias = expand_part(rows_low, cols_low, bias_high) + expand_part(
        rows_low, cols_low, bias_rest
    )
    return full_bias.reshape(
        full_bias.shape[0] * full_bias.shape[1], full_bias.shape[2] * full_bias.shape[3]
    )


def bias_gradient(grad_grid, window_span):
    tile_rows, tile_cols, padded_rows, padded_cols = grad_grid.shape
    by_rows = jnp.transpose(grad_grid, (0, 2, 1, 3)).reshape(
        tile_rows * padded_rows, tile_cols, padded_cols
    )
    by_rows = jnp.pad(by_rows, ((0, tile_rows), (0, 0), (0, 0)))
    by_rows = by_rows.reshape(tile_rows, padded_rows + 1, tile_cols, padded_cols)[:, :window_span]
    row_summed = jnp.sum(by_rows, axis=0).reshape(window_span, tile_cols * padded_cols)
    row_summed = jnp.pad(row_summed, ((0, 0), (0, tile_cols)))
    skewed = row_summed.reshape(window_span, tile_cols, padded_cols + 1)[:, :, :window_span]
    return jnp.sum(skewed, axis=1)


def allowed_pairs(table_rows, table_cols, cell_filled):
    row_inside = jnp.sum(table_rows, axis=2)
    col_inside = jnp.sum(table_cols, axis=2)
    joint = (
        row_inside[:, None, :, None] * col_inside[None, :, None, :] * cell_filled[None, None, :, :]
    )
    return joint.reshape(joint.shape[0] * joint.shape[1], joint.shape[2] * joint.shape[3]) > 0.5


def pick_tiles(extent, radius):
    cell_shape = (extent + 2 * radius, 3)
    position = lax.broadcasted_iota(jnp.int32, cell_shape, 0)
    tile_index = lax.broadcasted_iota(jnp.int32, cell_shape, 1)
    tile_of_cell = (position >= radius).astype(jnp.int32) + (position >= radius + extent).astype(
        jnp.int32
    )
    return (tile_of_cell == tile_index).astype(jnp.float32)


def neighbour_cells(nearby, tile_rows, tile_cols, radius):
    pick_rows = pick_tiles(tile_rows, radius)
    pick_cols = pick_tiles(tile_cols, radius)
    inner_rows = jnp.dot(pick_rows, nearby, precision=lax.Precision.HIGHEST)
    return jnp.dot(inner_rows, pick_cols.T, precision=lax.Precision.HIGHEST)


def head_slice(matrix, head_index, head_width):
    return lax.dynamic_slice_in_dim(matrix, head_index * head_width, head_width, 1)


def fold_columns(partials, radius):
    interior = partials.shape[2] - 2 * radius
    from_after = from_behind(partials[:, :, :radius].astype(jnp.bfloat16), "col", -1).astype(
        jnp.float32
    )
    from_before = from_behind(
        partials[:, :, radius + interior :].astype(jnp.bfloat16), "col", 1
    ).astype(jnp.float32)
    middle = partials[:, :, radius : radius + interior]
    middle = middle.at[:, :, :radius].add(from_before)
    return middle.at[:, :, interior - radius :].add(from_after)


def fold_rows(partials, radius):
    interior = partials.shape[1] - 2 * radius
    from_after = from_behind(partials[:, :radius].astype(jnp.bfloat16), "row", -1).astype(
        jnp.float32
    )
    from_before = from_behind(
        partials[:, radius + interior :].astype(jnp.bfloat16), "row", 1
    ).astype(jnp.float32)
    middle = partials[:, radius : radius + interior]
    middle = middle.at[:, :radius].add(from_before)
    return middle.at[:, interior - radius :].add(from_after)


def transposed_dot(left_matrix, right_matrix):
    return lax.dot_general(
        left_matrix, right_matrix, (((0,), (0,)), ((), ())), preferred_element_type=jnp.float32
    )


def rows_dot(left_matrix, right_matrix):
    return lax.dot_general(
        left_matrix, right_matrix, (((1,), (1,)), ((), ())), preferred_element_type=jnp.float32
    )


def shards(queries, keys, values, grad_out, rel_bias, occupied):
    tile_rows, tile_cols, model_width = queries.shape
    head_count = rel_bias.shape[0]
    window_span = rel_bias.shape[1]
    radius = (window_span - 1) // 2
    head_width = model_width // head_count
    score_scale = head_width ** (-0.5)
    padded_rows = tile_rows + 2 * radius
    padded_cols = tile_cols + 2 * radius
    query_count = tile_rows * tile_cols
    padded_count = padded_rows * padded_cols
    row_index = lax.axis_index("row")
    col_index = lax.axis_index("col")
    nearby = lax.dynamic_slice(jnp.pad(occupied, 1), (row_index, col_index), (3, 3)).astype(
        jnp.float32
    )
    own_tile = nearby[1, 1]
    cell_filled = neighbour_cells(nearby, tile_rows, tile_cols, radius)
    key_value_halo = with_halo(jnp.stack((keys, values)), (("row", 1), ("col", 2)), radius)
    key_matrix = key_value_halo[0].reshape(padded_count, model_width)
    value_matrix = key_value_halo[1].reshape(padded_count, model_width)
    query_matrix = queries.reshape(query_count, model_width)
    grad_matrix = grad_out.reshape(query_count, model_width)
    forward_rows = offset_table(tile_rows, padded_rows, 1, window_span)
    forward_cols = offset_table(tile_cols, padded_cols, 1, window_span)
    forward_allowed = allowed_pairs(forward_rows, forward_cols, cell_filled)
    partial_shape = (padded_count, model_width)

    def query_pass(head_index, carried):
        grad_query, grad_key, grad_value, log_total, delta_all, grad_bias = carried
        query_head = head_slice(query_matrix, head_index, head_width)
        key_head = head_slice(key_matrix, head_index, head_width)
        value_head = head_slice(value_matrix, head_index, head_width)
        grad_head = head_slice(grad_matrix, head_index, head_width)
        bias_head = lax.dynamic_index_in_dim(rel_bias, head_index, 0, keepdims=False)
        scores = rows_dot(query_head, key_head) * score_scale + expand_bias(
            forward_rows, forward_cols, bias_head
        )
        scores = jnp.where(forward_allowed, scores, -jnp.inf)
        row_max = jnp.max(scores, axis=1, keepdims=True)
        exponent = jnp.exp(scores - row_max)
        row_total = jnp.sum(exponent, axis=1, keepdims=True)
        weights = exponent / row_total
        grad_weights = rows_dot(grad_head, value_head)
        row_delta = jnp.sum(weights * grad_weights, axis=1, keepdims=True)
        grad_scores = weights * (grad_weights - row_delta)
        weights_low = weights.astype(jnp.bfloat16)
        grad_scores_low = grad_scores.astype(jnp.bfloat16)
        query_term = (
            jnp.dot(grad_scores_low, key_head, preferred_element_type=jnp.float32) * score_scale
        )
        grad_query = lax.dynamic_update_slice_in_dim(
            grad_query, query_term, head_index * head_width, 1
        )
        bias_term = bias_gradient(
            grad_scores.reshape(tile_rows, tile_cols, padded_rows, padded_cols), window_span
        )
        grad_bias = lax.dynamic_update_index_in_dim(grad_bias, bias_term, head_index, 0)
        log_total = lax.dynamic_update_slice_in_dim(
            log_total, row_max + jnp.log(row_total), head_index, 1
        )
        delta_all = lax.dynamic_update_slice_in_dim(delta_all, row_delta, head_index, 1)
        key_term = transposed_dot(grad_scores_low, query_head) * score_scale
        value_term = transposed_dot(weights_low, grad_head)
        grad_key = lax.dynamic_update_slice_in_dim(grad_key, key_term, head_index * head_width, 1)
        grad_value = lax.dynamic_update_slice_in_dim(
            grad_value, value_term, head_index * head_width, 1
        )
        return (grad_query, grad_key, grad_value, log_total, delta_all, grad_bias)

    initial = (
        jnp.zeros((query_count, model_width), jnp.float32),
        jnp.zeros(partial_shape, jnp.float32),
        jnp.zeros(partial_shape, jnp.float32),
        jnp.zeros((query_count, head_count), jnp.float32),
        jnp.zeros((query_count, head_count), jnp.float32),
        jnp.zeros((head_count, window_span, window_span), jnp.float32),
    )

    def run_queries():
        return lax.fori_loop(0, head_count, query_pass, initial)

    def skip_queries():
        return initial

    grad_query, grad_key, grad_value, log_total, delta_all, grad_bias = lax.cond(
        own_tile > 0.5, run_queries, skip_queries
    )
    bias_summed = lax.psum(grad_bias, ("row", "col"))
    query_grads = grad_query.astype(jnp.bfloat16).reshape(tile_rows, tile_cols, model_width)
    partials = jnp.stack((grad_key, grad_value)).reshape(2, padded_rows, padded_cols, model_width)
    owned_grads = fold_rows(fold_columns(partials, radius), radius)
    return (
        query_grads,
        owned_grads[0].astype(jnp.bfloat16),
        owned_grads[1].astype(jnp.bfloat16),
        bias_summed,
    )


def solution(mesh):
    placed = (
        P("row", "col", None),
        P("row", "col", None),
        P("row", "col", None),
        P("row", "col", None),
        P(),
        P(),
    )
    return jax.shard_map(
        shards,
        mesh=mesh,
        in_specs=placed,
        out_specs=(P("row", "col", None), P("row", "col", None), P("row", "col", None), P()),
        check_vma=False,
    )
```

profile of v0, /device:TPU:0, one launch (start us, length us, event | category | flops | bytes accessed | tf_op | source)
XLA Modules:
  0.0 246.2 jit_solution(10566615659084771039)
XLA Ops:
  0.6 1.0 pad_maximum_fusion.2
  1.6 1.3 collective-permute-start.1
  2.9 5.5 %collective-permute-start = (bf16[2,8,16,512]{3,2,1,0:T(8,128)(2,1)S(1)}, bf16[2,8,16,512]{3,2,1,0:T(8,128)(2,1)S(1)}, u32[]{:S(2)}, u32[]{:S(2)}) collective-permute-start(bf16[2,8,16,512]{3,2,1,0:T(8,128)(2,1)S(1)} %pad_maximum_fusion.2), channel_id=1, source_target_pairs={{0,8},{8,16},{16,24},{1,9},{9,17},{17,25},{2,10},{10,18},{18,26},{... | collective-permute-start | bytes 786440 | tf_op jit(solution)/shard_map/ppermute | solution.py:18
  8.5 0.8 fusion.52
  9.3 0.2 fusion.49
  9.4 4.2 %collective-permute-done.1 = bf16[2,8,16,512]{3,2,1,0:T(8,128)(2,1)S(1)} collective-permute-done((bf16[2,8,16,512]{3,2,1,0:T(8,128)(2,1)S(1)}, bf16[2,8,16,512]{3,2,1,0:T(8,128)(2,1)S(1)}, u32[]{:S(2)}, u32[]{:S(2)}) %collective-permute-start.1) | collective-permute-done | bytes 262176 | tf_op jit(solution)/shard_map/ppermute | solution.py:21
  13.7 0.3 collective-permute-done
  14.0 1.1 pad_maximum_fusion.1
  15.1 1.3 collective-permute-start.2
  16.4 1.3 collective-permute-start.3
  17.7 0.6 slice.176
  19.0 0.2 fusion.48
  19.2 2.8 %collective-permute-done.3 = bf16[2,24,8,512]{3,2,1,0:T(8,128)(2,1)S(1)} collective-permute-done((bf16[2,24,8,512]{3,2,1,0:T(8,128)(2,1)S(1)}, bf16[2,24,8,512]{3,2,1,0:T(8,128)(2,1)S(1)}, u32[]{:S(2)}, u32[]{:S(2)}) %collective-permute-start.3) | collective-permute-done | bytes 393248 | tf_op jit(solution)/shard_map/ppermute | solution.py:21
  22.1 0.2 pad_maximum_fusion
  22.3 2.7 %conditional.1 = (f32[8,17,17]{2,1,0:T(8,128)S(1)}, bf16[8,16,512]{2,1,0:T(8,128)(2,1)S(1)}, f32[1,24,32,512]{3,2,1,0:T(8,128)}, f32[1,24,32,512]{3,2,1,0:T(8,128)}) conditional(s32[]{:T(128)} %bitcast.7, () %tuple.69, (bf16[8,16,512]{2,1,0:T(8,128)(2,1)}, bf16[2,24,32,512]{3,2,1,0:T(8,128)(2,1)S(1)}, bf16[8,16,512]{2,1,0:T(8,128)(2,1)}, ...), branch_computations={%region_0.1_spmd, %region_1.11_spmd} | conditional | flops 72604152 | bytes 37085184 | solution.py:220
  22.3 1.4 stack.5.clone
  23.7 1.3 stack.5
  25.0 1.6 constant_dynamic-update-slice_fusion.1
  26.6 1.5 constant_dynamic-update-slice_fusion
  28.1 0.2 convert.13
  28.5 154.9 %collective-permute-start.4 = (bf16[2,24,8,512]{3,2,1,0:T(8,128)(2,1)S(1)}, bf16[2,24,8,512]{3,2,1,0:T(8,128)(2,1)S(1)}, u32[]{:S(2)}, u32[]{:S(2)}) collective-permute-start(bf16[2,24,8,512]{3,2,1,0:T(8,128)(2,1)S(1)} %get-tuple-element.623), channel_id=1, source_target_pairs={{0,1},{1,2},{2,3},{3,4},{4,5},{5,6},{6,7},{8,9},{9,10},{10,11},{11... | collective-permute-start | bytes 1179656 | tf_op jit(solution)/shard_map/ppermute | solution.py:10
  183.4 1.3 collective-permute-start.5
  184.7 0.1 slice.195
  184.8 0.1 fusion.43
  184.9 2.0 collective-permute-done.5
  187.0 0.2 fusion.42
  187.2 0.1 convert.14
  187.4 5.9 %collective-permute-start.6 = (bf16[2,8,16,512]{3,2,1,0:T(8,128)(2,1)S(1)}, bf16[2,8,16,512]{3,2,1,0:T(8,128)(2,1)S(1)}, u32[]{:S(2)}, u32[]{:S(2)}) collective-permute-start(bf16[2,8,16,512]{3,2,1,0:T(8,128)(2,1)S(1)} %get-tuple-element.624), channel_id=1, source_target_pairs={{0,8},{8,16},{16,24},{1,9},{9,17},{17,25},{2,10},{10,18},{18,26},{... | collective-permute-start | bytes 786440 | tf_op jit(solution)/shard_map/ppermute | solution.py:10
  193.3 1.3 collective-permute-start.7
  194.6 50.8 %psum.7 = f32[8,17,17]{2,0,1:T(8,128)} all-reduce(f32[8,17,17]{2,0,1:T(8,128)S(1)} %copy.61), channel_id=1, replica_groups=mesh['row'=4,'col'=8] {'row','col'}, use_global_device_ids=true, to_apply=%region_11.12 | all-reduce | flops 2312 | bytes 18496 | tf_op jit(solution)/shard_map/psum | solution.py:223
  245.4 0.1 fusion.45
  245.5 0.7 slice_bitcast_fusion
  (20 shorter events, 0.3 us)
Async XLA Ops:
  1.6 12.0 %collective-permute-start.1 = (bf16[2,8,16,512]{3,2,1,0:T(8,128)(2,1)S(1)}, bf16[2,8,16,512]{3,2,1,0:T(8,128)(2,1)S(1)}, u32[]{:S(2)}, u32[]{:S(2)}) collective-permute-start(bf16[2,8,16,512]{3,2,1,0:T(8,128)(2,1)S(1)} %pad_maximum_fusion.2), channel_id=1, source_target_pairs={{8,0},{16,8},{24,16},{9,1},{17,9},{25,17},{10,2},{18,10},{26,18},{... | collective-permute-start | bytes 786440 | tf_op jit(solution)/shard_map/ppermute | solution.py:21
  2.9 11.1 %collective-permute-start = (bf16[2,8,16,512]{3,2,1,0:T(8,128)(2,1)S(1)}, bf16[2,8,16,512]{3,2,1,0:T(8,128)(2,1)S(1)}, u32[]{:S(2)}, u32[]{:S(2)}) collective-permute-start(bf16[2,8,16,512]{3,2,1,0:T(8,128)(2,1)S(1)} %pad_maximum_fusion.2), channel_id=1, source_target_pairs={{0,8},{8,16},{16,24},{1,9},{9,17},{17,25},{2,10},{10,18},{18,26},{... | collective-permute-start | bytes 786440 | tf_op jit(solution)/shard_map/ppermute | solution.py:18
  9.4 12.6 %copy-start.3 = (bf16[8,16,512]{2,1,0:T(8,128)(2,1)S(1)}, bf16[8,16,512]{2,1,0:T(8,128)(2,1)}, u32[]{:S(2)}) copy-start(bf16[8,16,512]{2,1,0:T(8,128)(2,1)} %param.24) | copy-start | bytes 393220
  9.4 12.6 %copy-start.4 = (bf16[8,16,512]{2,1,0:T(8,128)(2,1)S(1)}, bf16[8,16,512]{2,1,0:T(8,128)(2,1)}, u32[]{:S(2)}) copy-start(bf16[8,16,512]{2,1,0:T(8,128)(2,1)} %param.23) | copy-start | bytes 393220
  15.1 4.1 %collective-permute-start.2 = (bf16[2,24,8,512]{3,2,1,0:T(8,128)(2,1)S(1)}, bf16[2,24,8,512]{3,2,1,0:T(8,128)(2,1)S(1)}, u32[]{:S(2)}, u32[]{:S(2)}) collective-permute-start(bf16[2,24,8,512]{3,2,1,0:T(8,128)(2,1)S(1)} %get-tuple-element.626), channel_id=1, source_target_pairs={{0,1},{1,2},{2,3},{3,4},{4,5},{5,6},{6,7},{8,9},{9,10},{10,11},{11... | collective-permute-start | bytes 1179656 | tf_op jit(solution)/shard_map/ppermute | solution.py:18
  16.4 5.6 %collective-permute-start.3 = (bf16[2,24,8,512]{3,2,1,0:T(8,128)(2,1)S(1)}, bf16[2,24,8,512]{3,2,1,0:T(8,128)(2,1)S(1)}, u32[]{:S(2)}, u32[]{:S(2)}) collective-permute-start(bf16[2,24,8,512]{3,2,1,0:T(8,128)(2,1)S(1)} %get-tuple-element.627), channel_id=1, source_target_pairs={{1,0},{2,1},{3,2},{4,3},{5,4},{6,5},{7,6},{9,8},{10,9},{11,10},{12... | collective-permute-start | bytes 1179656 | tf_op jit(solution)/shard_map/ppermute | solution.py:21
  25.0 1.6 copy-start.6
  28.5 156.4 %collective-permute-start.4 = (bf16[2,24,8,512]{3,2,1,0:T(8,128)(2,1)S(1)}, bf16[2,24,8,512]{3,2,1,0:T(8,128)(2,1)S(1)}, u32[]{:S(2)}, u32[]{:S(2)}) collective-permute-start(bf16[2,24,8,512]{3,2,1,0:T(8,128)(2,1)S(1)} %get-tuple-element.623), channel_id=1, source_target_pairs={{0,1},{1,2},{2,3},{3,4},{4,5},{5,6},{6,7},{8,9},{9,10},{10,11},{11... | collective-permute-start | bytes 1179656 | tf_op jit(solution)/shard_map/ppermute | solution.py:10
  183.4 3.6 %collective-permute-start.5 = (bf16[2,24,8,512]{3,2,1,0:T(8,128)(2,1)S(1)}, bf16[2,24,8,512]{3,2,1,0:T(8,128)(2,1)S(1)}, u32[]{:S(2)}, u32[]{:S(2)}) collective-permute-start(bf16[2,24,8,512]{3,2,1,0:T(8,128)(2,1)S(1)} %get-tuple-element.622), channel_id=1, source_target_pairs={{1,0},{2,1},{3,2},{4,3},{5,4},{6,5},{7,6},{9,8},{10,9},{11,10},{12... | collective-permute-start | bytes 1179656 | tf_op jit(solution)/shard_map/ppermute | solution.py:10
  187.4 58.0 %collective-permute-start.6 = (bf16[2,8,16,512]{3,2,1,0:T(8,128)(2,1)S(1)}, bf16[2,8,16,512]{3,2,1,0:T(8,128)(2,1)S(1)}, u32[]{:S(2)}, u32[]{:S(2)}) collective-permute-start(bf16[2,8,16,512]{3,2,1,0:T(8,128)(2,1)S(1)} %get-tuple-element.624), channel_id=1, source_target_pairs={{0,8},{8,16},{16,24},{1,9},{9,17},{17,25},{2,10},{10,18},{18,26},{... | collective-permute-start | bytes 786440 | tf_op jit(solution)/shard_map/ppermute | solution.py:10
  193.3 52.1 %collective-permute-start.7 = (bf16[2,8,16,512]{3,2,1,0:T(8,128)(2,1)S(1)}, bf16[2,8,16,512]{3,2,1,0:T(8,128)(2,1)S(1)}, u32[]{:S(2)}, u32[]{:S(2)}) collective-permute-start(bf16[2,8,16,512]{3,2,1,0:T(8,128)(2,1)S(1)} %get-tuple-element.625), channel_id=1, source_target_pairs={{8,0},{16,8},{24,16},{9,1},{17,9},{25,17},{10,2},{18,10},{26,18},{... | collective-permute-start | bytes 786440 | tf_op jit(solution)/shard_map/ppermute | solution.py:10
where the time goes:
time: 249 us; the launch traced here: 246 us
  starting transfers between devices  173 us (69%)
  blocking collectives  50.8 us (20%)
  waiting for transfers between devices  9.44 us (4%)
  local copies, waits for them, and re-layouts  7.44 us (3%)
  other arithmetic  3.82 us (2%)
    ppermute x4, starting transfers between devices, from_behind(): lax.ppermute(value, axis, [(source, source + steps) for source in range(f...  163 us
    psum x1, blocking collectives, shards(): bias_summed = lax.psum(grad_bias, ('row', 'col'))  50.8 us
    ppermute x2, waiting for transfers between devices, with_halo(): lax.ppermute(lax.slice_in_dim(block, 0, width, axis=dim), axis, backward)  7.05 us
    ppermute x2, starting transfers between devices, with_halo(): lax.ppermute(lax.slice_in_dim(block, block.shape[dim] - width, None, axis...  6.83 us
  transfers between devices with their start and end apart: 8, of which 4 were waited for; matrix products, arithmetic and copies ran while one was open for 1% of the time, Pallas kernels for 0%

commit v1 on v0

--- a/solution.py
+++ b/solution.py
@@ -220,7 +220,8 @@
     grad_query, grad_key, grad_value, log_total, delta_all, grad_bias = lax.cond(
         own_tile > 0.5, run_queries, skip_queries
     )
-    bias_summed = lax.psum(grad_bias, ("row", "col"))
+    parts = lax.all_gather(grad_bias, ("row", "col"))
+    bias_summed = jnp.sum(parts, axis=0)
     query_grads = grad_query.astype(jnp.bfloat16).reshape(tile_rows, tile_cols, model_width)
     partials = jnp.stack((grad_key, grad_value)).reshape(2, padded_rows, padded_cols, model_width)
     owned_grads = fold_rows(fold_columns(partials, radius), radius)

time: 249 us -> 259 us (1.040)
  blocking collectives: 50.8 us -> 59 us
    all_gather x0 -> x1, blocking collectives: none -> 59 us  [shards(): parts = lax.all_gather(grad_bias, ('row', 'col'))]
    psum x1 -> x0, blocking collectives: 50.8 us -> none  [shards(): bias_summed = lax.psum(grad_bias, ('row', 'col'))]
where the time goes in v1:
time: 259 us; the launch traced here: 256 us
  starting transfers between devices  173 us (67%)
  blocking collectives  59 us (23%)
  waiting for transfers between devices  9.37 us (4%)
  local copies, waits for them, and re-layouts  8.09 us (3%)
  other arithmetic  4.62 us (2%)
    ppermute x4, starting transfers between devices, from_behind(): lax.ppermute(value, axis, [(source, source + steps) for source in range(f...  164 us
    all_gather x1, blocking collectives, shards(): parts = lax.all_gather(grad_bias, ('row', 'col'))  59 us
    ppermute x2, waiting for transfers between devices, with_halo(): lax.ppermute(lax.slice_in_dim(block, 0, width, axis=dim), axis, backward)  7.05 us
    ppermute x2, starting transfers between devices, with_halo(): lax.ppermute(lax.slice_in_dim(block, block.shape[dim] - width, None, axis...  6.83 us
  transfers between devices with their start and end apart: 8, of which 4 were waited for; matrix products, arithmetic and copies ran while one was open for 1% of the time, Pallas kernels for 0%

profile of v1, /device:TPU:0, one launch (start us, length us, event | category | flops | bytes accessed | tf_op | source)
XLA Modules:
  0.0 256.0 jit_solution(1405224396193310682)
XLA Ops:
  0.6 1.0 pad_maximum_fusion.2
  1.6 1.3 collective-permute-start.1
  2.9 5.5 %collective-permute-start = (bf16[2,8,16,512]{3,2,1,0:T(8,128)(2,1)S(1)}, bf16[2,8,16,512]{3,2,1,0:T(8,128)(2,1)S(1)}, u32[]{:S(2)}, u32[]{:S(2)}) collective-permute-start(bf16[2,8,16,512]{3,2,1,0:T(8,128)(2,1)S(1)} %pad_maximum_fusion.2), channel_id=1, source_target_pairs={{0,8},{8,16},{16,24},{1,9},{9,17},{17,25},{2,10},{10,18},{18,26},{... | collective-permute-start | bytes 786440 | tf_op jit(solution)/shard_map/ppermute | solution.py:18
  8.5 0.8 fusion.52
  9.3 0.2 fusion.49
  9.4 4.2 %collective-permute-done.1 = bf16[2,8,16,512]{3,2,1,0:T(8,128)(2,1)S(1)} collective-permute-done((bf16[2,8,16,512]{3,2,1,0:T(8,128)(2,1)S(1)}, bf16[2,8,16,512]{3,2,1,0:T(8,128)(2,1)S(1)}, u32[]{:S(2)}, u32[]{:S(2)}) %collective-permute-start.1) | collective-permute-done | bytes 262176 | tf_op jit(solution)/shard_map/ppermute | solution.py:21
  13.7 0.3 collective-permute-done
  14.0 1.1 pad_maximum_fusion.1
  15.1 1.3 collective-permute-start.2
  16.4 1.3 collective-permute-start.3
  17.7 0.6 slice.176
  19.0 0.2 fusion.48
  19.2 2.8 %collective-permute-done.3 = bf16[2,24,8,512]{3,2,1,0:T(8,128)(2,1)S(1)} collective-permute-done((bf16[2,24,8,512]{3,2,1,0:T(8,128)(2,1)S(1)}, bf16[2,24,8,512]{3,2,1,0:T(8,128)(2,1)S(1)}, u32[]{:S(2)}, u32[]{:S(2)}) %collective-permute-start.3) | collective-permute-done | bytes 393248 | tf_op jit(solution)/shard_map/ppermute | solution.py:21
  22.1 0.2 pad_maximum_fusion
  22.3 3.4 %conditional.1 = (f32[8,17,17]{2,1,0:T(8,128)S(1)}, bf16[8,16,512]{2,1,0:T(8,128)(2,1)}, f32[1,24,32,512]{3,2,1,0:T(8,128)}, f32[1,24,32,512]{3,2,1,0:T(8,128)}) conditional(s32[]{:T(128)} %bitcast.7, () %tuple.69, (bf16[8,16,512]{2,1,0:T(8,128)(2,1)}, bf16[2,24,32,512]{3,2,1,0:T(8,128)(2,1)S(1)}, bf16[8,16,512]{2,1,0:T(8,128)(2,1)}, ...), branch_computations={%region_0.1_spmd, %region_1.11_spmd} | conditional | flops 72604152 | bytes 37085184 | solution.py:220
  22.3 0.7 reshape.255
  23.0 1.4 stack.5.clone
  24.3 1.3 stack.5
  25.7 1.5 constant_dynamic-update-slice_fusion.1
  27.2 1.5 constant_dynamic-update-slice_fusion
  28.7 0.2 convert.13
  29.1 155.1 %collective-permute-start.4 = (bf16[2,24,8,512]{3,2,1,0:T(8,128)(2,1)S(1)}, bf16[2,24,8,512]{3,2,1,0:T(8,128)(2,1)S(1)}, u32[]{:S(2)}, u32[]{:S(2)}) collective-permute-start(bf16[2,24,8,512]{3,2,1,0:T(8,128)(2,1)S(1)} %get-tuple-element.631), channel_id=1, source_target_pairs={{0,1},{1,2},{2,3},{3,4},{4,5},{5,6},{6,7},{8,9},{9,10},{10,11},{11... | collective-permute-start | bytes 1179656 | tf_op jit(solution)/shard_map/ppermute | solution.py:10
  184.1 1.3 collective-permute-start.5
  185.4 0.2 slice.195
  185.6 0.1 fusion.43
  185.8 2.0 collective-permute-done.5
  187.8 0.2 fusion.42
  188.1 5.9 %collective-permute-start.6 = (bf16[2,8,16,512]{3,2,1,0:T(8,128)(2,1)S(1)}, bf16[2,8,16,512]{3,2,1,0:T(8,128)(2,1)S(1)}, u32[]{:S(2)}, u32[]{:S(2)}) collective-permute-start(bf16[2,8,16,512]{3,2,1,0:T(8,128)(2,1)S(1)} %get-tuple-element.632), channel_id=1, source_target_pairs={{0,8},{8,16},{16,24},{1,9},{9,17},{17,25},{2,10},{10,18},{18,26},{... | collective-permute-start | bytes 786440 | tf_op jit(solution)/shard_map/ppermute | solution.py:10
  194.1 1.3 collective-permute-start.7
  195.4 59.0 %all-gather = f32[256,17,17]{2,0,1:T(8,128)S(1)} all-gather(f32[8,17,17]{2,0,1:T(8,128)S(1)} %copy.61), channel_id=2, replica_groups=mesh['row'=4,'col'=8] {'row','col'}, dimensions={0}, use_global_device_ids=true | all-gather | bytes 305184 | tf_op jit(solution)/shard_map/all_gather | solution.py:223
  254.4 0.8 bitcast_reduce_fusion
  255.3 0.7 slice_bitcast_fusion
  (19 shorter events, 0.5 us)
Async XLA Ops:
  1.6 12.0 %collective-permute-start.1 = (bf16[2,8,16,512]{3,2,1,0:T(8,128)(2,1)S(1)}, bf16[2,8,16,512]{3,2,1,0:T(8,128)(2,1)S(1)}, u32[]{:S(2)}, u32[]{:S(2)}) collective-permute-start(bf16[2,8,16,512]{3,2,1,0:T(8,128)(2,1)S(1)} %pad_maximum_fusion.2), channel_id=1, source_target_pairs={{8,0},{16,8},{24,16},{9,1},{17,9},{25,17},{10,2},{18,10},{26,18},{... | collective-permute-start | bytes 786440 | tf_op jit(solution)/shard_map/ppermute | solution.py:21
  2.9 11.1 %collective-permute-start = (bf16[2,8,16,512]{3,2,1,0:T(8,128)(2,1)S(1)}, bf16[2,8,16,512]{3,2,1,0:T(8,128)(2,1)S(1)}, u32[]{:S(2)}, u32[]{:S(2)}) collective-permute-start(bf16[2,8,16,512]{3,2,1,0:T(8,128)(2,1)S(1)} %pad_maximum_fusion.2), channel_id=1, source_target_pairs={{0,8},{8,16},{16,24},{1,9},{9,17},{17,25},{2,10},{10,18},{18,26},{... | collective-permute-start | bytes 786440 | tf_op jit(solution)/shard_map/ppermute | solution.py:18
  9.4 12.6 %copy-start.3 = (bf16[8,16,512]{2,1,0:T(8,128)(2,1)S(1)}, bf16[8,16,512]{2,1,0:T(8,128)(2,1)}, u32[]{:S(2)}) copy-start(bf16[8,16,512]{2,1,0:T(8,128)(2,1)} %param.24) | copy-start | bytes 393220
  9.4 12.6 %copy-start.4 = (bf16[8,16,512]{2,1,0:T(8,128)(2,1)S(1)}, bf16[8,16,512]{2,1,0:T(8,128)(2,1)}, u32[]{:S(2)}) copy-start(bf16[8,16,512]{2,1,0:T(8,128)(2,1)} %param.23) | copy-start | bytes 393220
  15.1 4.1 %collective-permute-start.2 = (bf16[2,24,8,512]{3,2,1,0:T(8,128)(2,1)S(1)}, bf16[2,24,8,512]{3,2,1,0:T(8,128)(2,1)S(1)}, u32[]{:S(2)}, u32[]{:S(2)}) collective-permute-start(bf16[2,24,8,512]{3,2,1,0:T(8,128)(2,1)S(1)} %get-tuple-element.634), channel_id=1, source_target_pairs={{0,1},{1,2},{2,3},{3,4},{4,5},{5,6},{6,7},{8,9},{9,10},{10,11},{11... | collective-permute-start | bytes 1179656 | tf_op jit(solution)/shard_map/ppermute | solution.py:18
  16.4 5.6 %collective-permute-start.3 = (bf16[2,24,8,512]{3,2,1,0:T(8,128)(2,1)S(1)}, bf16[2,24,8,512]{3,2,1,0:T(8,128)(2,1)S(1)}, u32[]{:S(2)}, u32[]{:S(2)}) collective-permute-start(bf16[2,24,8,512]{3,2,1,0:T(8,128)(2,1)S(1)} %get-tuple-element.635), channel_id=1, source_target_pairs={{1,0},{2,1},{3,2},{4,3},{5,4},{6,5},{7,6},{9,8},{10,9},{11,10},{12... | collective-permute-start | bytes 1179656 | tf_op jit(solution)/shard_map/ppermute | solution.py:21
  29.1 156.6 %collective-permute-start.4 = (bf16[2,24,8,512]{3,2,1,0:T(8,128)(2,1)S(1)}, bf16[2,24,8,512]{3,2,1,0:T(8,128)(2,1)S(1)}, u32[]{:S(2)}, u32[]{:S(2)}) collective-permute-start(bf16[2,24,8,512]{3,2,1,0:T(8,128)(2,1)S(1)} %get-tuple-element.631), channel_id=1, source_target_pairs={{0,1},{1,2},{2,3},{3,4},{4,5},{5,6},{6,7},{8,9},{9,10},{10,11},{11... | collective-permute-start | bytes 1179656 | tf_op jit(solution)/shard_map/ppermute | solution.py:10
  184.1 3.6 %collective-permute-start.5 = (bf16[2,24,8,512]{3,2,1,0:T(8,128)(2,1)S(1)}, bf16[2,24,8,512]{3,2,1,0:T(8,128)(2,1)S(1)}, u32[]{:S(2)}, u32[]{:S(2)}) collective-permute-start(bf16[2,24,8,512]{3,2,1,0:T(8,128)(2,1)S(1)} %get-tuple-element.630), channel_id=1, source_target_pairs={{1,0},{2,1},{3,2},{4,3},{5,4},{6,5},{7,6},{9,8},{10,9},{11,10},{12... | collective-permute-start | bytes 1179656 | tf_op jit(solution)/shard_map/ppermute | solution.py:10
  188.1 67.0 %collective-permute-start.6 = (bf16[2,8,16,512]{3,2,1,0:T(8,128)(2,1)S(1)}, bf16[2,8,16,512]{3,2,1,0:T(8,128)(2,1)S(1)}, u32[]{:S(2)}, u32[]{:S(2)}) collective-permute-start(bf16[2,8,16,512]{3,2,1,0:T(8,128)(2,1)S(1)} %get-tuple-element.632), channel_id=1, source_target_pairs={{0,8},{8,16},{16,24},{1,9},{9,17},{17,25},{2,10},{10,18},{18,26},{... | collective-permute-start | bytes 786440 | tf_op jit(solution)/shard_map/ppermute | solution.py:10
  194.1 61.1 %collective-permute-start.7 = (bf16[2,8,16,512]{3,2,1,0:T(8,128)(2,1)S(1)}, bf16[2,8,16,512]{3,2,1,0:T(8,128)(2,1)S(1)}, u32[]{:S(2)}, u32[]{:S(2)}) collective-permute-start(bf16[2,8,16,512]{3,2,1,0:T(8,128)(2,1)S(1)} %get-tuple-element.633), channel_id=1, source_target_pairs={{8,0},{16,8},{24,16},{9,1},{17,9},{25,17},{10,2},{18,10},{26,18},{... | collective-permute-start | bytes 786440 | tf_op jit(solution)/shard_map/ppermute | solution.py:10
